TPU v7x, 256 devices: a whole 4x4x8 slice. The times are simulated.
256 devices in a mesh: row: 16 (over y, z_lo), col: 16 (over x, z_hi, core).
Axes of the slice: x: 4, y: 4, z: 8 (z_hi: 2, z_lo: 4; z = z_hi * 4 + z_lo), core: 2. Of those that a mesh axis runs over, the one named last changes fastest.
Arguments:
- features: float32 [65536, 128], P(('col', 'row')), may hold values from -6 to 6
- weight: float32 [128, 128], replicated, may hold values from -4 to 4
- bias_vector: float32 [128], replicated, may hold values from -4 to 4
- out_grad: float32 [65536, 128], P(('row', 'col')), may hold values from -6 to 6
- adj_tiles: int32 [16, 16, 128, 128, 128], P('row', 'col'), may hold values 0 or 1
- tile_slots: int32 [16, 16, 128], P('row', 'col'), may hold values from 0 to 1023, as said below
- tile_counts: int32 [16, 16], P('row', 'col'), may hold values from 17 to 128, as said below
Outputs:
- activated: float32 [65536, 128], P(('row', 'col'))
- feature_grad: float32 [65536, 128], P(('col', 'row'))
- weight_grad: float32 [128, 128], replicated
- bias_grad: float32 [128], replicated
Inputs may be any that keep to these rules, and one draw needn't show every extreme that they name: `tile_slots`: each block's slots name distinct positions r * 32 + c of its 32 x 32 tiles. Some block is full in every draw; slots from tile_counts on are ignored.
All inputs are finite; a program needn't handle non-finite values. No bound on the sum of `adj_tiles` on one device may be relied on, other than what follows from the above.
Results may differ from a plain program's by a relative error of at most 0.0003.
Values sent between devices are 32-bit elements; how exact they have to be, the bound alone decides.
A program may use at most 128 MiB of HBM per device.

v0:
```python
import jax
import jax.numpy as jnp
from jax import lax
from jax.sharding import PartitionSpec as P

TILE = 128


def dense_step(aggregated, weight, bias_vector, cotangent):
    preact = jnp.dot(aggregated, weight, precision=lax.Precision.HIGHEST) + bias_vector
    logistic = jax.nn.sigmoid(preact)
    activated = preact * logistic
    pre_grad = cotangent * logistic * (1.0 + preact * (1.0 - logistic))
    weight_part = jnp.dot(aggregated.T, pre_grad, precision=lax.Precision.HIGHEST)
    bias_part = jnp.sum(pre_grad, axis=0)
    back_rows = jnp.dot(pre_grad, weight.T, precision=lax.Precision.HIGHEST)
    return (activated, weight_part, bias_part, back_rows)


def local(features, weight, bias_vector, out_grad, adj_tiles, tile_slots, tile_counts):
    row_count = lax.axis_size("row")
    col_count = lax.axis_size("col")
    node_rows = features.shape[0]
    width = features.shape[1]
    tile_rows = node_rows * col_count // TILE
    tile_cols = node_rows * row_count // TILE
    adjacency = adj_tiles[0, 0].astype(jnp.float32)
    slots = tile_slots[0, 0]
    slot_total = slots.shape[0]
    live_mask = (jnp.arange(slot_total) < tile_counts[0, 0]).astype(jnp.float32)
    tile_row = slots // tile_cols
    tile_col = slots % tile_cols
    row_select = (tile_row[:, None] == jnp.arange(tile_rows)[None, :]).astype(
        jnp.float32
    ) * live_mask[:, None]
    col_select = (tile_col[:, None] == jnp.arange(tile_cols)[None, :]).astype(
        jnp.float32
    ) * live_mask[:, None]
    dst_partial = jnp.dot(
        row_select.T, jnp.sum(adjacency, axis=2), precision=lax.Precision.HIGHEST
    ).reshape(-1)
    src_partial = jnp.dot(
        col_select.T, jnp.sum(adjacency, axis=1), precision=lax.Precision.HIGHEST
    ).reshape(-1)
    src_scale = lax.rsqrt(
        1.0 + lax.psum_scatter(src_partial, "row", scatter_dimension=0, tiled=True)
    )
    scaled = features * src_scale[:, None]
    gathered = lax.all_gather(scaled, "row", axis=0, tiled=True)
    taken = jnp.take(gathered.reshape(tile_cols, TILE, width), tile_col, axis=0)
    product = jnp.einsum(
        "kab,kbh->kah",
        adjacency,
        taken,
        precision=lax.Precision.HIGHEST,
        preferred_element_type=jnp.float32,
    )
    partial_value = jnp.einsum(
        "kr,kah->rah",
        row_select,
        product,
        precision=lax.Precision.HIGHEST,
        preferred_element_type=jnp.float32,
    ).reshape(tile_rows * TILE, width)
    dst_scale = lax.rsqrt(
        1.0 + lax.psum_scatter(dst_partial, "col", scatter_dimension=0, tiled=True)
    )
    aggregated = (
        lax.psum_scatter(partial_value, "col", scatter_dimension=0, tiled=True) * dst_scale[:, None]
    )
    activated, weight_part, bias_part, back_rows = dense_step(
        aggregated, weight, bias_vector, out_grad
    )
    weight_grad, bias_grad = lax.psum((weight_part, bias_part), ("row", "col"))
    row_grads = lax.all_gather(back_rows * dst_scale[:, None], "col", axis=0, tiled=True)
    taken_back = jnp.take(row_grads.reshape(tile_rows, TILE, width), tile_row, axis=0)
    product_back = jnp.einsum(
        "kab,kah->kbh",
        adjacency,
        taken_back,
        precision=lax.Precision.HIGHEST,
        preferred_element_type=jnp.float32,
    )
    partial_back = jnp.einsum(
        "kc,kbh->cbh",
        col_select,
        product_back,
        precision=lax.Precision.HIGHEST,
        preferred_element_type=jnp.float32,
    ).reshape(tile_cols * TILE, width)
    feature_grad = (
        lax.psum_scatter(partial_back, "row", scatter_dimension=0, tiled=True) * src_scale[:, None]
    )
    return (activated, feature_grad, weight_grad, bias_grad)


def solution(mesh):
    return jax.shard_map(
        local,
        mesh=mesh,
        in_specs=(
            P(("col", "row"), None),
            P(),
            P(),
            P(("row", "col"), None),
            P("row", "col", None, None, None),
            P("row", "col", None),
            P("row", "col"),
        ),
        out_specs=(P(("row", "col"), None), P(("col", "row"), None), P(), P()),
        check_vma=False,
    )
```

profile of v0, /device:TPU:1, one launch (start us, length us, event | category | flops | bytes accessed | tf_op | source)
XLA Modules:
  0.0 764.2 jit_solution(688655162839533169)
XLA Ops:
  7.9 1.3 dynamic-slice
  9.9 5.7 convert_reduce_fusion
  15.8 68.3 %all-reduce = f32[4096]{0:T(1024)S(1)} all-reduce(f32[4096]{0:T(1024)S(1)} %convolution_bitcast_fusion.1), channel_id=2, replica_groups=mesh['row'=16,'col'=16] {'row'}, use_global_device_ids=true, to_apply=%region_1.2.clone | all-reduce | flops 4096 | bytes 32768
  85.1 89.2 %all-gather.3.cloned.1.call-done = f32[4096,128]{1,0:T(8,128)} async-done(((f32[256,128]{1,0:T(8,128)}), f32[4096,128]{1,0:T(8,128)}) %all-gather.3.cloned.1.call-update) | async-done | bytes 2097168 | tf_op jit(solution)/shard_map/all_gather | solution.py:49
  174.3 5.9 gather_fusion
  180.1 21.5 %fusion.12 = f32[128,128,128]{1,2,0:T(8,128)} fusion(s32[1,1,128,128,128]{4,3,2,1,0:T(8,128)} %param.13, f32[128,128,128]{2,1,0:T(8,128)} %gather_fusion, pred[128]{0:T(512)(128)(4,1)S(1)} %get-tuple-element.14), kind=kOutput, calls=%fused_computation.16 | convolution fusion | flops 3225419776 | bytes 25165952 | tf_op jit(solution)/shard_map/kab,kbh->kah/dot_general | solution.py:51
  201.7 9.3 %copy.18 = f32[128,128,128]{2,0,1:T(8,128)} copy(f32[128,128,128]{1,2,0:T(8,128)} %fusion.12) | data formatting | bytes 16777216 | tf_op jit(solution)/shard_map/kab,kbh->kah/dot_general | solution.py:51
  211.0 6.8 fusion.30
  217.7 2.6 copy.19
  221.8 87.6 %all-reduce.1 = f32[4096]{0:T(1024)S(1)} all-reduce(f32[4096]{0:T(1024)S(1)} %convolution_bitcast_fusion), channel_id=4, replica_groups=mesh['row'=16,'col'=16] {'col'}, use_global_device_ids=true, to_apply=%region_4.6.clone | all-reduce | flops 4096 | bytes 32768
  309.5 4.8 reduce-scatter.3.cloned.1.call-done
  314.3 1.9 fusion.52
  316.2 0.9 convolution_multiply_fusion
  317.2 62.5 %all-gather.5.cloned.1.call-done = f32[4096,128]{1,0:T(8,128)} async-done(((f32[256,128]{1,0:T(8,128)}), f32[4096,128]{1,0:T(8,128)}) %all-gather.5.cloned.1.call-update) | async-done | bytes 2097168 | tf_op jit(solution)/shard_map/all_gather | solution.py:75
  379.7 5.9 gather_fusion.1
  385.6 19.7 %fusion.17 = f32[128,128,128]{1,2,0:T(8,128)} fusion(s32[1,1,128,128,128]{4,3,2,1,0:T(8,128)} %param.13, f32[128,128,128]{2,1,0:T(8,128)} %gather_fusion.1, pred[128]{0:T(512)(128)(4,1)S(1)} %get-tuple-element.9), kind=kOutput, calls=%fused_computation.17 | convolution fusion | flops 3225419776 | bytes 25165952 | tf_op jit(solution)/shard_map/kab,kah->kbh/dot_general | solution.py:77
  405.3 9.3 %copy.21 = f32[128,128,128]{2,0,1:T(8,128)} copy(f32[128,128,128]{1,2,0:T(8,128)} %fusion.17) | data formatting | bytes 16777216 | tf_op jit(solution)/shard_map/kab,kah->kbh/dot_general | solution.py:77
  414.6 6.8 fusion.31
  421.4 2.6 copy.22
  424.0 76.6 %psum.15 = f32[128]{0:T(128)} all-reduce(f32[128]{0:T(128)S(1)} %get-tuple-element.7), channel_id=1, replica_groups=mesh['row'=16,'col'=16] {'row','col'}, use_global_device_ids=true, to_apply=%region_8.10 | all-reduce | flops 128 | bytes 1024 | tf_op jit(solution)/shard_map/psum | solution.py:74
  500.6 1.1 fusion.23
  501.8 1.7 broadcast_multiply_fusion
  503.4 252.8 %all-reduce.4.cloned.1.call-done = f32[128,128]{1,0:T(8,128)} async-done(((f32[128,128]{1,0:T(8,128)}), f32[128,128]{1,0:T(8,128)}) %all-reduce.4.cloned.1.call-update) | async-done | bytes 65552 | tf_op jit(solution)/shard_map/psum | solution.py:74
  756.2 1.5 copy.27
  (36 shorter events, 2.2 us)
Async XLA Ops:
  7.2 307.1 %copy-start = (f32[128,128]{1,0:T(8,128)S(1)}, f32[128,128]{1,0:T(8,128)}, u32[]{:S(2)}) copy-start(f32[128,128]{1,0:T(8,128)} %param.10) | copy-start | bytes 196612
  7.2 8.4 %copy-start.3 = (s32[1,1,128]{2,1,0:T(1,128)S(1)}, s32[1,1,128]{2,1,0:T(1,128)}, u32[]{:S(2)}) copy-start(s32[1,1,128]{2,1,0:T(1,128)} %param.14) | copy-start | bytes 1540
  7.2 77.0 %copy-start.1 = (f32[256,128]{1,0:T(8,128)S(1)}, f32[256,128]{1,0:T(8,128)}, u32[]{:S(2)}) copy-start(f32[256,128]{1,0:T(8,128)} %param.9) | copy-start | bytes 393220
  7.2 167.1 %all-gather.3.cloned.1.call-start = ((), (), s32[]{:S(2)}) async-start(), calls=%async_computation.2 | async-start | bytes 2228224 | tf_op jit(solution)/shard_map/all_gather | solution.py:49
  85.0 229.3 %reduce-scatter.3.cloned.1.call-start = ((), (), s32[]{:S(2)}) async-start(), calls=%async_computation.3 | async-start | bytes 2228224 | tf_op jit(solution)/shard_map/reduce_scatter | solution.py:69
  211.0 9.4 %copy-start.6 = (u32[256]{0:T(256)S(1)}, u32[256]{0:T(256)}, u32[]{:S(2)}) copy-start(u32[256]{0:T(256)} %constant.56) | copy-start | bytes 3076
  211.0 103.3 %copy-start.4 = (f32[256,128]{1,0:T(8,128)S(1)}, f32[256,128]{1,0:T(8,128)}, u32[]{:S(2)}) copy-start(f32[256,128]{1,0:T(8,128)} %param.12) | copy-start | bytes 393220
  211.0 103.3 %copy-start.5 = (f32[128]{0:T(128)S(1)}, f32[128]{0:T(128)}, u32[]{:S(2)}) copy-start(f32[128]{0:T(128)} %param.11) | copy-start | bytes 1540
  220.3 159.4 %all-gather.5.cloned.1.call-start = ((), (), s32[]{:S(2)}) async-start(), calls=%async_computation.4 | async-start | bytes 2228224 | tf_op jit(solution)/shard_map/all_gather | solution.py:75
  317.2 184.6 %reduce-scatter.5.cloned.1.call-start = ((), (), s32[]{:S(2)}) async-start(), calls=%async_computation.5 | async-start | bytes 2228224 | tf_op jit(solution)/shard_map/reduce_scatter | solution.py:92
  414.6 86.0 %copy-start.2 = (f32[256,128]{1,0:T(8,128)S(1)}, f32[256,128]{1,0:T(8,128)}, u32[]{:S(2)}) copy-start(f32[256,128]{1,0:T(8,128)} %reduce-scatter.3.cloned.1.call-done) | copy-start | bytes 393220
  424.0 332.2 %all-reduce.4.cloned.1.call-start = ((), (), s32[]{:S(2)}) async-start(), calls=%async_computation.6 | async-start | bytes 131072 | tf_op jit(solution)/shard_map/psum | solution.py:74
Sparse Core Ops, SparseCore 0:
  85.1 89.0 all-gather.2
  220.5 93.7 reduce-scatter.2
  317.5 62.1 all-gather.4
  424.1 77.1 reduce-scatter.4
  507.3 248.8 all-reduce.3
where the time goes:
time: 765 us; the launch traced here: 764 us
  waiting for transfers between devices  409 us (53%)
  blocking collectives  232 us (30%)
  matrix products  59 us (8%)
  local copies, waits for them, and re-layouts  38.9 us (5%)
  between operations  15.9 us (2%)
  other arithmetic  8.34 us (1%)
    psum x1, waiting for transfers between devices, local(): weight_grad, bias_grad = lax.psum((weight_part, bias_part), ('row', 'col'))  253 us
    unnamed x2, blocking collectives  156 us
    all_gather x1, waiting for transfers between devices, local(): gathered = lax.all_gather(scaled, 'row', axis=0, tiled=True)  89.2 us
    psum x1, blocking collectives, local(): weight_grad, bias_grad = lax.psum((weight_part, bias_part), ('row', 'col'))  76.6 us
    all_gather x1, waiting for transfers between devices, local(): lax.all_gather(back_rows * dst_scale[:, None], 'col', axis=0, tiled=True)  62.5 us
    dot_general x1, matrix products, local(): jnp.einsum('kab,kbh->kah', adjacency, taken, precision=lax.Precision.HIGH...  21.5 us
    dot_general x1, matrix products, local(): jnp.einsum('kab,kah->kbh', adjacency, taken_back, precision=lax.Precision...  19.7 us
  transfers between devices with their start and end apart: 5, of which 4 were waited for; matrix products, arithmetic and copies ran while one was open for 0% of the time, Pallas kernels for 0%

commit v1 on v0

--- a/solution.py
+++ b/solution.py
@@ -71,7 +71,7 @@
     activated, weight_part, bias_part, back_rows = dense_step(
         aggregated, weight, bias_vector, out_grad
     )
-    weight_grad, bias_grad = lax.psum((weight_part, bias_part), ("row", "col"))
+    weight_grad, bias_grad = lax.psum(lax.psum((weight_part, bias_part), "row"), "col")
     row_grads = lax.all_gather(back_rows * dst_scale[:, None], "col", axis=0, tiled=True)
     taken_back = jnp.take(row_grads.reshape(tile_rows, TILE, width), tile_row, axis=0)
     product_back = jnp.einsum(

time: 765 us -> 794 us (1.038)
  waiting for transfers between devices: 409 us -> 431 us
    reduce_scatter x1, waiting for transfers between devices: 0.02 us -> 90.8 us  [local(): lax.psum_scatter(partial_back, 'row', scatter_dimension=0, tiled=True)]
    psum x1 -> x2, waiting for transfers between devices: 253 us -> 185 us  [the longest x1 174 us: local(): lax.psum(lax.psum((weight_part, bias_part), 'row'), 'col')]
    psum x1 -> x2, blocking collectives: 76.6 us -> 82.9 us  [the longest x1 49.6 us: local(): lax.psum(lax.psum((weight_part, bias_part), 'row'), 'col')]
  transfers between devices with their start and end apart: 5 -> 6, of which waited for: 4 -> 6; matrix products, arithmetic and copies ran while one was open for 0% -> 6% of each run, Pallas kernels for 0% -> 0%
where the time goes in v1:
time: 794 us; the launch traced here: 793 us
  waiting for transfers between devices  431 us (54%)
  blocking collectives  239 us (30%)
  matrix products  59.9 us (8%)
  local copies, waits for them, and re-layouts  38.9 us (5%)
  between operations  16.2 us (2%)
  other arithmetic  8.34 us (1%)
    psum x1, waiting for transfers between devices, local(): lax.psum(lax.psum((weight_part, bias_part), 'row'), 'col')  174 us
    unnamed x2, blocking collectives  156 us
    reduce_scatter x1, waiting for transfers between devices, local(): lax.psum_scatter(partial_back, 'row', scatter_dimension=0, tiled=True)  90.8 us
    all_gather x1, waiting for transfers between devices, local(): gathered = lax.all_gather(scaled, 'row', axis=0, tiled=True)  89.2 us
    all_gather x1, waiting for transfers between devices, local(): lax.all_gather(back_rows * dst_scale[:, None], 'col', axis=0, tiled=True)  60 us
    psum x1, blocking collectives, local(): lax.psum(lax.psum((weight_part, bias_part), 'row'), 'col')  49.6 us
    psum x1, blocking collectives, local(): lax.psum((weight_part, bias_part), 'row')  33.3 us
    dot_general x1, matrix products, local(): jnp.einsum('kab,kbh->kah', adjacency, taken, precision=lax.Precision.HIGH...  21.5 us
  transfers between devices with their start and end apart: 6, of which 6 were waited for; matrix products, arithmetic and copies ran while one was open for 6% of the time, Pallas kernels for 0%

profile of v1, /device:TPU:1, one launch (start us, length us, event | category | flops | bytes accessed | tf_op | source)
XLA Modules:
  0.0 793.1 jit_solution(15905517699055009396)
XLA Ops:
  9.9 5.7 convert_reduce_fusion
  15.8 68.3 %all-reduce = f32[4096]{0:T(1024)S(1)} all-reduce(f32[4096]{0:T(1024)S(1)} %convolution_bitcast_fusion.1), channel_id=2, replica_groups=mesh['row'=16,'col'=16] {'row'}, use_global_device_ids=true, to_apply=%region_1.2.clone | all-reduce | flops 4096 | bytes 32768
  85.1 89.2 %all-gather.3.cloned.1.call-done = f32[4096,128]{1,0:T(8,128)} async-done(((f32[256,128]{1,0:T(8,128)}), f32[4096,128]{1,0:T(8,128)}) %all-gather.3.cloned.1.call-update) | async-done | bytes 2097168 | tf_op jit(solution)/shard_map/all_gather | solution.py:49
  174.3 5.9 gather_fusion
  180.1 21.5 %fusion.12 = f32[128,128,128]{1,2,0:T(8,128)} fusion(s32[1,1,128,128,128]{4,3,2,1,0:T(8,128)} %param.13, f32[128,128,128]{2,1,0:T(8,128)} %gather_fusion, pred[128]{0:T(512)(128)(4,1)S(1)} %get-tuple-element.14), kind=kOutput, calls=%fused_computation.16 | convolution fusion | flops 3225419776 | bytes 25165952 | tf_op jit(solution)/shard_map/kab,kbh->kah/dot_general | solution.py:51
  201.7 9.3 %copy.18 = f32[128,128,128]{2,0,1:T(8,128)} copy(f32[128,128,128]{1,2,0:T(8,128)} %fusion.12) | data formatting | bytes 16777216 | tf_op jit(solution)/shard_map/kab,kbh->kah/dot_general | solution.py:51
  211.0 6.8 fusion.30
  217.8 2.6 copy.19
  221.8 87.6 %all-reduce.1 = f32[4096]{0:T(1024)S(1)} all-reduce(f32[4096]{0:T(1024)S(1)} %convolution_bitcast_fusion), channel_id=4, replica_groups=mesh['row'=16,'col'=16] {'col'}, use_global_device_ids=true, to_apply=%region_4.6.clone | all-reduce | flops 4096 | bytes 32768
  309.5 5.2 reduce-scatter.3.cloned.1.call-done
  314.7 1.9 fusion.52
  317.7 2.0 fusion.23
  319.8 60.0 %all-gather.5.cloned.1.call-done = f32[4096,128]{1,0:T(8,128)} async-done(((f32[256,128]{1,0:T(8,128)}), f32[4096,128]{1,0:T(8,128)}) %all-gather.5.cloned.1.call-update) | async-done | bytes 2097168 | tf_op jit(solution)/shard_map/all_gather | solution.py:75
  379.7 5.9 gather_fusion.1
  385.6 19.7 %fusion.17 = f32[128,128,128]{1,2,0:T(8,128)} fusion(s32[1,1,128,128,128]{4,3,2,1,0:T(8,128)} %param.13, f32[128,128,128]{2,1,0:T(8,128)} %gather_fusion.1, pred[128]{0:T(512)(128)(4,1)S(1)} %get-tuple-element.9), kind=kOutput, calls=%fused_computation.17 | convolution fusion | flops 3225419776 | bytes 25165952 | tf_op jit(solution)/shard_map/kab,kah->kbh/dot_general | solution.py:77
  405.4 9.3 %copy.21 = f32[128,128,128]{2,0,1:T(8,128)} copy(f32[128,128,128]{1,2,0:T(8,128)} %fusion.17) | data formatting | bytes 16777216 | tf_op jit(solution)/shard_map/kab,kah->kbh/dot_general | solution.py:77
  414.7 6.7 fusion.31
  421.4 2.6 copy.22
  424.0 33.3 %psum.30 = f32[128]{0:T(128)S(1)} all-reduce(f32[128]{0:T(128)S(1)} %get-tuple-element.7), channel_id=1, replica_groups=mesh['row'=16,'col'=16] {'row'}, use_global_device_ids=true, to_apply=%region_9.11 | all-reduce | flops 128 | bytes 1024 | tf_op jit(solution)/shard_map/psum | solution.py:74
  457.3 49.6 %psum.31 = f32[128]{0:T(128)} all-reduce(f32[128]{0:T(128)S(1)} %psum.30), channel_id=1, replica_groups=mesh['row'=16,'col'=16] {'col'}, use_global_device_ids=true, to_apply=%region_10.12 | all-reduce | flops 128 | bytes 1024 | tf_op jit(solution)/shard_map/psum | solution.py:74
  507.0 11.8 %all-reduce.5.cloned.1.call-done = f32[128,128]{1,0:T(8,128)} async-done(((f32[128,128]{1,0:T(8,128)}), f32[128,128]{1,0:T(8,128)}) %all-reduce.5.cloned.1.call-update) | async-done | bytes 65552 | tf_op jit(solution)/shard_map/psum | solution.py:74
  518.8 90.8 %reduce-scatter.5.cloned.1.call-done = f32[256,128]{1,0:T(8,128)} async-done(((f32[4096,128]{1,0:T(8,128)}), f32[256,128]{1,0:T(8,128)}) %reduce-scatter.5.cloned.1.call-update) | async-done | bytes 131088 | tf_op jit(solution)/shard_map/reduce_scatter | solution.py:92
  609.6 1.7 broadcast_multiply_fusion
  611.3 173.5 %all-reduce.7.cloned.1.call-done = f32[128,128]{1,0:T(8,128)} async-done(((f32[128,128]{1,0:T(8,128)}), f32[128,128]{1,0:T(8,128)}) %all-reduce.7.cloned.1.call-update) | async-done | bytes 65552 | tf_op jit(solution)/shard_map/psum | solution.py:74
  (38 shorter events, 5.9 us)
Async XLA Ops:
  7.2 307.6 %copy-start = (f32[128,128]{1,0:T(8,128)S(1)}, f32[128,128]{1,0:T(8,128)}, u32[]{:S(2)}) copy-start(f32[128,128]{1,0:T(8,128)} %param.10) | copy-start | bytes 196612
  7.2 8.4 %copy-start.2 = (s32[1,1,128]{2,1,0:T(1,128)S(1)}, s32[1,1,128]{2,1,0:T(1,128)}, u32[]{:S(2)}) copy-start(s32[1,1,128]{2,1,0:T(1,128)} %param.14) | copy-start | bytes 1540
  7.2 77.0 %copy-start.1 = (f32[256,128]{1,0:T(8,128)S(1)}, f32[256,128]{1,0:T(8,128)}, u32[]{:S(2)}) copy-start(f32[256,128]{1,0:T(8,128)} %param.9) | copy-start | bytes 393220
  7.2 167.1 %all-gather.3.cloned.1.call-start = ((), (), s32[]{:S(2)}) async-start(), calls=%async_computation.2 | async-start | bytes 2228224 | tf_op jit(solution)/shard_map/all_gather | solution.py:49
  85.0 229.7 %reduce-scatter.3.cloned.1.call-start = ((), (), s32[]{:S(2)}) async-start(), calls=%async_computation.3 | async-start | bytes 2228224 | tf_op jit(solution)/shard_map/reduce_scatter | solution.py:69
  211.0 9.4 %copy-start.5 = (u32[256]{0:T(256)S(1)}, u32[256]{0:T(256)}, u32[]{:S(2)}) copy-start(u32[256]{0:T(256)} %constant.56) | copy-start | bytes 3076
  211.0 103.7 %copy-start.3 = (f32[256,128]{1,0:T(8,128)S(1)}, f32[256,128]{1,0:T(8,128)}, u32[]{:S(2)}) copy-start(f32[256,128]{1,0:T(8,128)} %param.12) | copy-start | bytes 393220
  211.0 103.7 %copy-start.4 = (f32[128]{0:T(128)S(1)}, f32[128]{0:T(128)}, u32[]{:S(2)}) copy-start(f32[128]{0:T(128)} %param.11) | copy-start | bytes 1540
  220.3 159.4 %all-gather.5.cloned.1.call-start = ((), (), s32[]{:S(2)}) async-start(), calls=%async_computation.4 | async-start | bytes 2228224 | tf_op jit(solution)/shard_map/all_gather | solution.py:75
  317.6 201.1 %all-reduce.5.cloned.1.call-start = ((), (), s32[]{:S(2)}) async-start(), calls=%async_computation.6 | async-start | bytes 131072 | tf_op jit(solution)/shard_map/psum | solution.py:74
  319.7 289.9 %reduce-scatter.5.cloned.1.call-start = ((), (), s32[]{:S(2)}) async-start(), calls=%async_computation.5 | async-start | bytes 2228224 | tf_op jit(solution)/shard_map/reduce_scatter | solution.py:92
  424.0 360.8 %all-reduce.7.cloned.1.call-start = ((), (), s32[]{:S(2)}) async-start(), calls=%async_computation.7 | async-start | bytes 131072 | tf_op jit(solution)/shard_map/psum | solution.py:74
Sparse Core Ops, SparseCore 0:
  85.1 89.0 all-gather.2
  220.5 94.2 reduce-scatter.2
  318.0 61.7 all-gather.4
  382.8 135.8 all-reduce.4
  521.1 88.4 reduce-scatter.4
  612.1 172.6 all-reduce.6
